TPU v7x, 32 devices: a whole 2x2x4 slice. The times are simulated.
32 devices in a mesh: bin: 4 (over x, core), slab: 8 (over z, y).
Axes of the slice: x: 2, y: 2, z: 4, core: 2. Of those that a mesh axis runs over, the one named last changes fastest.
Arguments:
- volumes: float32 [8, 32, 64, 512], P('bin', 'slab'), may hold values from -6 to 6
- attenuation: float32 [8, 3], replicated, may hold values from 0.2 to 1.2
- penalty: float32 [1], replicated, may hold values from 0.2 to 0.4
- tv_weight: float32 [1], replicated, may hold values from 0.3 to 0.8
Outputs:
- materials: float32 [3, 32, 64, 512], P(None, ('bin', 'slab'))
All inputs are finite; a program needn't handle non-finite values.
Results may differ from a plain program's by a relative error of at most 0.0001.
Values sent between devices are 32-bit elements; how exact they have to be, the bound alone decides.
No kernel may reach another device: no remote copies, remote signals or barrier semaphores. Data moves between devices by JAX's collectives and lax.ppermute only.
A program may use at most 64 MiB of HBM per device.

v0:
```python
import jax
import jax.numpy as jnp
from jax import lax
from jax.sharding import PartitionSpec as P

ITERS = 3


def from_behind(x, axis, by):
    peers = lax.axis_size(axis)
    pairs = [(i, i + by) for i in range(peers) if 0 <= i + by < peers]
    return lax.ppermute(x, axis, pairs)


def inverse_three(matrix):
    cofactor = [
        [
            matrix[(row + 1) % 3, (col + 1) % 3] * matrix[(row + 2) % 3, (col + 2) % 3]
            - matrix[(row + 1) % 3, (col + 2) % 3] * matrix[(row + 2) % 3, (col + 1) % 3]
            for col in range(3)
        ]
        for row in range(3)
    ]
    determinant = (
        matrix[0, 0] * cofactor[0][0]
        + matrix[0, 1] * cofactor[0][1]
        + matrix[0, 2] * cofactor[0][2]
    )
    return [[cofactor[col][row] / determinant for col in range(3)] for row in range(3)]


def normal_inverse(attenuation, penalty_value):
    gram = jnp.dot(attenuation.T, attenuation, precision=lax.Precision.HIGHEST)
    gram = gram + 12.0 * penalty_value * jnp.eye(3, dtype=jnp.float32)
    return inverse_three(gram)


def apply_inverse(inverse, fields):
    return jnp.stack(
        [
            inverse[row][0] * fields[0] + inverse[row][1] * fields[1] + inverse[row][2] * fields[2]
            for row in range(3)
        ]
    )


def project(attenuation, volumes):
    return jnp.einsum("km,kzyx->mzyx", attenuation, volumes, precision=lax.Precision.HIGHEST)


def gradient(field):
    interior_z = (lax.axis_index("bin") < lax.axis_size("bin") - 1).astype(jnp.float32)
    interior_y = (lax.axis_index("slab") < lax.axis_size("slab") - 1).astype(jnp.float32)
    below = from_behind(field[:, :1], "bin", -1)
    after = from_behind(field[:, :, :1], "slab", -1)
    along_z = jnp.concatenate(
        [field[:, 1:] - field[:, :-1], (below - field[:, -1:]) * interior_z], 1
    )
    along_y = jnp.concatenate(
        [field[:, :, 1:] - field[:, :, :-1], (after - field[:, :, -1:]) * interior_y], 2
    )
    along_x = jnp.concatenate(
        [field[:, :, :, 1:] - field[:, :, :, :-1], jnp.zeros_like(field[:, :, :, :1])], 3
    )
    return [along_z, along_y, along_x]


def divergence(parts):
    above = from_behind(parts[0][:, -1:], "bin", 1)
    before = from_behind(parts[1][:, :, -1:], "slab", 1)
    total = parts[0] - jnp.concatenate([above, parts[0][:, :-1]], 1)
    total = total + (parts[1] - jnp.concatenate([before, parts[1][:, :, :-1]], 2))
    total = total + (
        parts[2]
        - jnp.concatenate([jnp.zeros_like(parts[2][:, :, :, :1]), parts[2][:, :, :, :-1]], 3)
    )
    return total


def clip_group(parts, threshold):
    squares = (
        jnp.sum(parts[0] * parts[0], axis=0)
        + jnp.sum(parts[1] * parts[1], axis=0)
        + jnp.sum(parts[2] * parts[2], axis=0)
    )
    scale = threshold / jnp.maximum(jnp.sqrt(squares), threshold)
    return [part * scale[None] for part in parts]


def on_device(volumes, attenuation, penalty, tv_weight):
    penalty_value = penalty[0]
    threshold = tv_weight[0] / penalty_value
    inverse = normal_inverse(attenuation, penalty_value)
    cube = lax.all_to_all(
        lax.all_to_all(volumes, "slab", split_axis=2, concat_axis=1, tiled=True),
        "bin",
        split_axis=1,
        concat_axis=0,
        tiled=True,
    )
    data = project(attenuation, cube)
    field = apply_inverse(inverse, data)
    dual = clip_group(gradient(field), threshold)
    step_parts = [2.0 * part for part in dual]
    for turn in range(ITERS):
        field = apply_inverse(
            inverse, data + 12.0 * penalty_value * field + penalty_value * divergence(step_parts)
        )
        if turn < ITERS - 1:
            grads = gradient(field)
            fresh = clip_group([grads[index] + dual[index] for index in range(3)], threshold)
            step_parts = [2.0 * fresh[index] - dual[index] for index in range(3)]
            dual = fresh
    return lax.all_to_all(field, "slab", split_axis=1, concat_axis=2, tiled=True)


def solution(mesh):
    placed = (P("bin", "slab", None, None), P(), P(), P())
    return jax.shard_map(
        on_device,
        mesh=mesh,
        in_specs=placed,
        out_specs=P(None, ("bin", "slab"), None, None),
        check_vma=False,
    )
```

profile of v0, /device:TPU:0, one launch (start us, length us, event | category | flops | bytes accessed | tf_op | source)
XLA Modules:
  0.0 149.0 jit_solution(16900868698549911127)
XLA Ops:
  0.0 1.9 %copy.18 = f32[2,4,64,512]{3,1,0,2:T(4,128)S(1)} copy(f32[2,4,64,512]{3,2,1,0:T(8,128)} %param.4) | data formatting | bytes 2097152 | tf_op args[0]
  1.9 32.9 %all_to_all.48 = f32[2,4,64,512]{3,1,0,2:T(4,128)S(1)} all-to-all(f32[2,4,64,512]{3,1,0,2:T(4,128)S(1)} %copy.18), channel_id=1, replica_groups=mesh['bin'=4,'slab'=8] {'slab'}, dimensions={2} | all-to-all | bytes 2097152 | tf_op jit(solution)/shard_map/all_to_all | solution.py:95
  34.8 0.6 copy.31
  35.4 0.1 copy.20
  35.5 1.1 copy.21
  36.6 3.5 %all-to-all-start.1 = ((f32[2,32,8,512]{3,2,0,1:T(8,128)}), f32[2,32,8,512]{3,2,0,1:T(8,128)S(1)}, u32[]{:S(2)}, u32[]{:S(2)}) async-start(f32[2,32,8,512]{3,2,0,1:T(8,128)} %copy.21), calls=%async_computation.1 | async-start | bytes 2097152 | tf_op jit(solution)/shard_map/all_to_all | solution.py:94
  40.8 0.1 convolution_add_fusion
  40.9 0.7 fusion.21
  67.1 0.8 copy.23
  67.9 0.7 all_to_all.42
  68.7 1.0 fusion.19
  69.7 0.6 multiply_add_fusion.11
  70.3 0.4 pad_maximum_fusion
  70.7 0.1 slice_subtract_fusion.7
  70.8 0.3 slice_subtract_fusion.2
  71.2 1.3 collective-permute-start.1
  72.5 0.1 slice_subtract_fusion.8
  72.6 1.3 collective-permute-start
  73.9 0.4 multiply_reduce_fusion.6
  74.2 3.3 %collective-permute-done.1 = f32[3,8,1,512]{3,0,2,1:T(4,128)S(1)} collective-permute-done((f32[3,8,1,512]{3,0,2,1:T(4,128)S(1)}, f32[3,8,1,512]{3,0,2,1:T(4,128)S(1)}, u32[]{:S(2)}, u32[]{:S(2)}) %collective-permute-start.1) | collective-permute-done | bytes 49184 | tf_op jit(solution)/shard_map/ppermute | solution.py:12
  77.5 0.4 multiply_reduce_fusion.7
  78.0 0.4 multiply_reduce_fusion.8
  78.4 0.5 fusion.12
  78.9 2.6 %collective-permute-start.2 = (f32[3,1,8,512]{3,0,2,1:T(4,128)S(1)}, f32[3,1,8,512]{3,0,2,1:T(4,128)S(1)}, u32[]{:S(2)}, u32[]{:S(2)}) collective-permute-start(f32[3,1,8,512]{3,0,2,1:T(4,128)S(1)} %slice.331), channel_id=1, source_target_pairs={{0,8},{8,16},{16,24},{1,9},{9,17},{17,25},{2,10},{10,18},{18,26},{... | collective-permute-start | bytes 147464 | tf_op jit(solution)/shard_map/ppermute | solution.py:12
  81.5 4.4 %collective-permute-start.3 = (f32[3,8,1,512]{3,0,2,1:T(4,128)S(1)}, f32[3,8,1,512]{3,0,2,1:T(4,128)S(1)}, u32[]{:S(2)}, u32[]{:S(2)}) collective-permute-start(f32[3,8,1,512]{3,0,2,1:T(4,128)S(1)} %slice.333), channel_id=1, source_target_pairs={{0,1},{1,2},{2,3},{3,4},{4,5},{5,6},{6,7},{8,9},{9,10},{10,11},{11... | collective-permute-start | bytes 147464 | tf_op jit(solution)/shard_map/ppermute | solution.py:12
  86.1 0.1 slice.332
  86.2 2.3 %collective-permute-done.3 = f32[3,8,1,512]{3,0,2,1:T(4,128)S(1)} collective-permute-done((f32[3,8,1,512]{3,0,2,1:T(4,128)S(1)}, f32[3,8,1,512]{3,0,2,1:T(4,128)S(1)}, u32[]{:S(2)}, u32[]{:S(2)}) %collective-permute-start.3) | collective-permute-done | bytes 49184 | tf_op jit(solution)/shard_map/ppermute | solution.py:12
  88.4 0.9 fusion.3
  89.3 0.6 multiply_add_fusion.8
  90.0 0.4 pad_maximum_fusion.3
  90.4 0.1 slice_subtract_fusion.5
  90.5 0.3 slice_subtract_fusion.1
  90.8 1.3 collective-permute-start.5
  92.1 0.1 slice_subtract_fusion.6
  92.2 1.5 collective-permute-start.4
  93.7 3.9 %collective-permute-done.5 = f32[3,8,1,512]{3,0,2,1:T(4,128)S(1)} collective-permute-done((f32[3,8,1,512]{3,0,2,1:T(4,128)S(1)}, f32[3,8,1,512]{3,0,2,1:T(4,128)S(1)}, u32[]{:S(2)}, u32[]{:S(2)}) %collective-permute-start.5) | collective-permute-done | bytes 49184 | tf_op jit(solution)/shard_map/ppermute | solution.py:12
  97.6 1.7 %multiply_reduce_fusion.3 = (f32[8,8,512]{2,1,0:T(8,128)S(1)}, f32[3,8,8,512]{3,0,2,1:T(4,128)S(1)}, f32[8,8,512]{2,1,0:T(8,128)S(1)}, f32[3,8,8,512]{3,0,2,1:T(...) fusion(f32[8,8,512]{2,1,0:T(8,128)S(1)} %maximum_divide_fusion.2, ...), kind=kLoop, calls=%fused_computation.43 | loop fusion | flops 1474560 | bytes 4061696 | tf_op jit(solution)/shard_map/reduce_sum | solution.py:84
  99.4 0.7 multiply_subtract_fusion.3
  100.2 2.3 %collective-permute-start.6 = (f32[3,1,8,512]{3,0,2,1:T(4,128)S(1)}, f32[3,1,8,512]{3,0,2,1:T(4,128)S(1)}, u32[]{:S(2)}, u32[]{:S(2)}) collective-permute-start(f32[3,1,8,512]{3,0,2,1:T(4,128)S(1)} %slice.349), channel_id=1, source_target_pairs={{0,8},{8,16},{16,24},{1,9},{9,17},{17,25},{2,10},{10,18},{18,26},{... | collective-permute-start | bytes 147464 | tf_op jit(solution)/shard_map/ppermute | solution.py:12
  102.4 5.0 %collective-permute-start.7 = (f32[3,8,1,512]{3,0,2,1:T(4,128)S(1)}, f32[3,8,1,512]{3,0,2,1:T(4,128)S(1)}, u32[]{:S(2)}, u32[]{:S(2)}) collective-permute-start(f32[3,8,1,512]{3,0,2,1:T(4,128)S(1)} %slice.351), channel_id=1, source_target_pairs={{0,1},{1,2},{2,3},{3,4},{4,5},{5,6},{6,7},{8,9},{9,10},{10,11},{11... | collective-permute-start | bytes 147464 | tf_op jit(solution)/shard_map/ppermute | solution.py:12
  107.4 0.1 slice.352
  107.5 0.1 slice.350
  107.6 1.7 %collective-permute-done.7 = f32[3,8,1,512]{3,0,2,1:T(4,128)S(1)} collective-permute-done((f32[3,8,1,512]{3,0,2,1:T(4,128)S(1)}, f32[3,8,1,512]{3,0,2,1:T(4,128)S(1)}, u32[]{:S(2)}, u32[]{:S(2)}) %collective-permute-start.7) | collective-permute-done | bytes 49184 | tf_op jit(solution)/shard_map/ppermute | solution.py:12
  109.3 0.8 fusion.7
  110.2 0.6 multiply_add_fusion.5
  110.8 0.4 pad_maximum_fusion.4
  111.2 0.1 slice_subtract_fusion.3
  111.3 0.3 slice_subtract_fusion
  111.6 1.3 collective-permute-start.9
  112.9 0.1 slice_subtract_fusion.4
  113.1 1.3 collective-permute-start.8
  114.4 4.1 %collective-permute-done.9 = f32[3,8,1,512]{3,0,2,1:T(4,128)S(1)} collective-permute-done((f32[3,8,1,512]{3,0,2,1:T(4,128)S(1)}, f32[3,8,1,512]{3,0,2,1:T(4,128)S(1)}, u32[]{:S(2)}, u32[]{:S(2)}) %collective-permute-start.9) | collective-permute-done | bytes 49184 | tf_op jit(solution)/shard_map/ppermute | solution.py:12
  118.5 1.4 multiply_reduce_fusion.1
  120.0 0.7 multiply_subtract_fusion
  120.7 1.5 %collective-permute-start.10 = (f32[3,1,8,512]{3,0,2,1:T(4,128)S(1)}, f32[3,1,8,512]{3,0,2,1:T(4,128)S(1)}, u32[]{:S(2)}, u32[]{:S(2)}) collective-permute-start(f32[3,1,8,512]{3,0,2,1:T(4,128)S(1)} %slice.367), channel_id=1, source_target_pairs={{0,8},{8,16},{16,24},{1,9},{9,17},{17,25},{2,10},{10,18},{18,26},{... | collective-permute-start | bytes 147464 | tf_op jit(solution)/shard_map/ppermute | solution.py:12
  122.3 5.2 %collective-permute-start.11 = (f32[3,8,1,512]{3,0,2,1:T(4,128)S(1)}, f32[3,8,1,512]{3,0,2,1:T(4,128)S(1)}, u32[]{:S(2)}, u32[]{:S(2)}) collective-permute-start(f32[3,8,1,512]{3,0,2,1:T(4,128)S(1)} %slice.369), channel_id=1, source_target_pairs={{0,1},{1,2},{2,3},{3,4},{4,5},{5,6},{6,7},{8,9},{9,10},{10,11},{11... | collective-permute-start | bytes 147464 | tf_op jit(solution)/shard_map/ppermute | solution.py:12
  127.4 0.1 slice.370
  127.6 1.7 %collective-permute-done.11 = f32[3,8,1,512]{3,0,2,1:T(4,128)S(1)} collective-permute-done((f32[3,8,1,512]{3,0,2,1:T(4,128)S(1)}, f32[3,8,1,512]{3,0,2,1:T(4,128)S(1)}, u32[]{:S(2)}, u32[]{:S(2)}) %collective-permute-start.11) | collective-permute-done | bytes 49184 | tf_op jit(solution)/shard_map/ppermute | solution.py:12
  129.3 0.9 fusion.11
  130.2 0.6 multiply_add_fusion.2
  130.8 0.4 pad_maximum_fusion.5
  131.2 0.1 copy.24
  131.3 16.9 %all_to_all.49 = f32[3,8,8,512]{3,2,0,1:T(8,128)S(1)} all-to-all(f32[3,8,8,512]{3,2,0,1:T(8,128)S(1)} %copy.24), channel_id=1, replica_groups=mesh['bin'=4,'slab'=8] {'slab'}, dimensions={1} | all-to-all | bytes 786432 | tf_op jit(solution)/shard_map/all_to_all | solution.py:114
  148.2 0.8 copy.32
  (32 shorter events, 0.7 us)
Async XLA Ops:
  0.0 40.8 %copy-start = (f32[8,3]{0,1:T(4,128)S(1)}, f32[8,3]{0,1:T(4,128)}, u32[]{:S(2)}) copy-start(f32[8,3]{0,1:T(4,128)} %param.5) | copy-start | bytes 292
  36.6 30.5 %all-to-all-start.1 = ((f32[2,32,8,512]{3,2,0,1:T(8,128)}), f32[2,32,8,512]{3,2,0,1:T(8,128)S(1)}, u32[]{:S(2)}, u32[]{:S(2)}) async-start(f32[2,32,8,512]{3,2,0,1:T(8,128)} %copy.21), calls=%async_computation.1 | async-start | bytes 2097152 | tf_op jit(solution)/shard_map/all_to_all | solution.py:94
  71.2 6.4 %collective-permute-start.1 = (f32[3,8,1,512]{3,0,2,1:T(4,128)S(1)}, f32[3,8,1,512]{3,0,2,1:T(4,128)S(1)}, u32[]{:S(2)}, u32[]{:S(2)}) collective-permute-start(f32[3,8,1,512]{3,0,2,1:T(4,128)S(1)} %slice.327), channel_id=1, source_target_pairs={{1,0},{2,1},{3,2},{4,3},{5,4},{6,5},{7,6},{9,8},{10,9},{11,10},{12... | collective-permute-start | bytes 147464 | tf_op jit(solution)/shard_map/ppermute | solution.py:12
  72.6 5.3 %collective-permute-start = (f32[3,1,8,512]{3,0,2,1:T(4,128)S(1)}, f32[3,1,8,512]{3,0,2,1:T(4,128)S(1)}, u32[]{:S(2)}, u32[]{:S(2)}) collective-permute-start(f32[3,1,8,512]{3,0,2,1:T(4,128)S(1)} %slice.323), channel_id=1, source_target_pairs={{8,0},{16,8},{24,16},{9,1},{17,9},{25,17},{10,2},{18,10},{26,18},{... | collective-permute-start | bytes 147464 | tf_op jit(solution)/shard_map/ppermute | solution.py:12
  78.9 7.2 %collective-permute-start.2 = (f32[3,1,8,512]{3,0,2,1:T(4,128)S(1)}, f32[3,1,8,512]{3,0,2,1:T(4,128)S(1)}, u32[]{:S(2)}, u32[]{:S(2)}) collective-permute-start(f32[3,1,8,512]{3,0,2,1:T(4,128)S(1)} %slice.331), channel_id=1, source_target_pairs={{0,8},{8,16},{16,24},{1,9},{9,17},{17,25},{2,10},{10,18},{18,26},{... | collective-permute-start | bytes 147464 | tf_op jit(solution)/shard_map/ppermute | solution.py:12
  81.5 6.9 %collective-permute-start.3 = (f32[3,8,1,512]{3,0,2,1:T(4,128)S(1)}, f32[3,8,1,512]{3,0,2,1:T(4,128)S(1)}, u32[]{:S(2)}, u32[]{:S(2)}) collective-permute-start(f32[3,8,1,512]{3,0,2,1:T(4,128)S(1)} %slice.333), channel_id=1, source_target_pairs={{0,1},{1,2},{2,3},{3,4},{4,5},{5,6},{6,7},{8,9},{9,10},{10,11},{11... | collective-permute-start | bytes 147464 | tf_op jit(solution)/shard_map/ppermute | solution.py:12
  90.8 6.8 %collective-permute-start.5 = (f32[3,8,1,512]{3,0,2,1:T(4,128)S(1)}, f32[3,8,1,512]{3,0,2,1:T(4,128)S(1)}, u32[]{:S(2)}, u32[]{:S(2)}) collective-permute-start(f32[3,8,1,512]{3,0,2,1:T(4,128)S(1)} %slice.345), channel_id=1, source_target_pairs={{1,0},{2,1},{3,2},{4,3},{5,4},{6,5},{7,6},{9,8},{10,9},{11,10},{12... | collective-permute-start | bytes 147464 | tf_op jit(solution)/shard_map/ppermute | solution.py:12
  92.2 5.4 %collective-permute-start.4 = (f32[3,1,8,512]{3,0,2,1:T(4,128)S(1)}, f32[3,1,8,512]{3,0,2,1:T(4,128)S(1)}, u32[]{:S(2)}, u32[]{:S(2)}) collective-permute-start(f32[3,1,8,512]{3,0,2,1:T(4,128)S(1)} %slice.341), channel_id=1, source_target_pairs={{8,0},{16,8},{24,16},{9,1},{17,9},{25,17},{10,2},{18,10},{26,18},{... | collective-permute-start | bytes 147464 | tf_op jit(solution)/shard_map/ppermute | solution.py:12
  100.2 7.5 %collective-permute-start.6 = (f32[3,1,8,512]{3,0,2,1:T(4,128)S(1)}, f32[3,1,8,512]{3,0,2,1:T(4,128)S(1)}, u32[]{:S(2)}, u32[]{:S(2)}) collective-permute-start(f32[3,1,8,512]{3,0,2,1:T(4,128)S(1)} %slice.349), channel_id=1, source_target_pairs={{0,8},{8,16},{16,24},{1,9},{9,17},{17,25},{2,10},{10,18},{18,26},{... | collective-permute-start | bytes 147464 | tf_op jit(solution)/shard_map/ppermute | solution.py:12
  102.4 6.9 %collective-permute-start.7 = (f32[3,8,1,512]{3,0,2,1:T(4,128)S(1)}, f32[3,8,1,512]{3,0,2,1:T(4,128)S(1)}, u32[]{:S(2)}, u32[]{:S(2)}) collective-permute-start(f32[3,8,1,512]{3,0,2,1:T(4,128)S(1)} %slice.351), channel_id=1, source_target_pairs={{0,1},{1,2},{2,3},{3,4},{4,5},{5,6},{6,7},{8,9},{9,10},{10,11},{11... | collective-permute-start | bytes 147464 | tf_op jit(solution)/shard_map/ppermute | solution.py:12
  111.6 6.8 %collective-permute-start.9 = (f32[3,8,1,512]{3,0,2,1:T(4,128)S(1)}, f32[3,8,1,512]{3,0,2,1:T(4,128)S(1)}, u32[]{:S(2)}, u32[]{:S(2)}) collective-permute-start(f32[3,8,1,512]{3,0,2,1:T(4,128)S(1)} %slice.363), channel_id=1, source_target_pairs={{1,0},{2,1},{3,2},{4,3},{5,4},{6,5},{7,6},{9,8},{10,9},{11,10},{12... | collective-permute-start | bytes 147464 | tf_op jit(solution)/shard_map/ppermute | solution.py:12
  113.1 5.4 %collective-permute-start.8 = (f32[3,1,8,512]{3,0,2,1:T(4,128)S(1)}, f32[3,1,8,512]{3,0,2,1:T(4,128)S(1)}, u32[]{:S(2)}, u32[]{:S(2)}) collective-permute-start(f32[3,1,8,512]{3,0,2,1:T(4,128)S(1)} %slice.359), channel_id=1, source_target_pairs={{8,0},{16,8},{24,16},{9,1},{17,9},{25,17},{10,2},{18,10},{26,18},{... | collective-permute-start | bytes 147464 | tf_op jit(solution)/shard_map/ppermute | solution.py:12
  120.7 6.9 %collective-permute-start.10 = (f32[3,1,8,512]{3,0,2,1:T(4,128)S(1)}, f32[3,1,8,512]{3,0,2,1:T(4,128)S(1)}, u32[]{:S(2)}, u32[]{:S(2)}) collective-permute-start(f32[3,1,8,512]{3,0,2,1:T(4,128)S(1)} %slice.367), channel_id=1, source_target_pairs={{0,8},{8,16},{16,24},{1,9},{9,17},{17,25},{2,10},{10,18},{18,26},{... | collective-permute-start | bytes 147464 | tf_op jit(solution)/shard_map/ppermute | solution.py:12
  122.3 7.1 %collective-permute-start.11 = (f32[3,8,1,512]{3,0,2,1:T(4,128)S(1)}, f32[3,8,1,512]{3,0,2,1:T(4,128)S(1)}, u32[]{:S(2)}, u32[]{:S(2)}) collective-permute-start(f32[3,8,1,512]{3,0,2,1:T(4,128)S(1)} %slice.369), channel_id=1, source_target_pairs={{0,1},{1,2},{2,3},{3,4},{4,5},{5,6},{6,7},{8,9},{9,10},{10,11},{11... | collective-permute-start | bytes 147464 | tf_op jit(solution)/shard_map/ppermute | solution.py:12
where the time goes:
time: 150 us; the launch traced here: 149 us
  blocking collectives  49.8 us (33%)
  starting transfers between devices  32.5 us (22%)
  between operations  26.7 us (18%)
  waiting for transfers between devices  16.9 us (11%)
  other arithmetic  14.6 us (10%)
  local copies, waits for them, and re-layouts  7.48 us (5%)
    all_to_all x1, blocking collectives, on_device(): lax.all_to_all(volumes, 'slab', split_axis=2, concat_axis=1, tiled=True)  32.9 us
    ppermute x12, starting transfers between devices, from_behind(): return lax.ppermute(x, axis, pairs)  28.9 us
    all_to_all x1, blocking collectives, on_device(): lax.all_to_all(field, 'slab', split_axis=1, concat_axis=2, tiled=True)  16.9 us
    ppermute x12, waiting for transfers between devices, from_behind(): return lax.ppermute(x, axis, pairs)  16.9 us
    all_to_all x1, starting transfers between devices, on_device(): lax.all_to_all(lax.all_to_all(volumes, 'slab', split_axis=2, concat_axis=...  3.51 us
  transfers between devices with their start and end apart: 13, of which 6 were waited for; matrix products, arithmetic and copies ran while one was open for 2% of the time, Pallas kernels for 0%

commit v1 on v0

--- a/solution.py
+++ b/solution.py
@@ -4,6 +4,12 @@
 from jax.sharding import PartitionSpec as P
 
 ITERS = 3
+
+
+def exchange_blocks(x, axis, split, join):
+    cells = jnp.split(x, lax.axis_size(axis), axis=split)
+    received = lax.all_to_all(jnp.stack(cells), axis, 0, 0)
+    return jnp.concatenate(received, axis=join)
 
 
 def from_behind(x, axis, by):
@@ -92,11 +98,7 @@
     threshold = tv_weight[0] / penalty_value
     inverse = normal_inverse(attenuation, penalty_value)
     cube = lax.all_to_all(
-        lax.all_to_all(volumes, "slab", split_axis=2, concat_axis=1, tiled=True),
-        "bin",
-        split_axis=1,
-        concat_axis=0,
-        tiled=True,
+        exchange_blocks(volumes, "slab", 2, 1), "bin", split_axis=1, concat_axis=0, tiled=True
     )
     data = project(attenuation, cube)
     field = apply_inverse(inverse, data)

time: 150 us -> 155 us (1.033)
  local copies, waits for them, and re-layouts: 7.48 us -> 12.3 us
    unnamed x3 -> x9, local copies, waits for them, and re-layouts: 1.92 us -> 6.43 us
    all_to_all x5 -> x3, local copies, waits for them, and re-layouts: 3.31 us -> 1.62 us  [the longest x2 1.53 us: on_device(): lax.all_to_all(exchange_blocks(volumes, 'slab', 2, 1), 'bin', split_axis=...]
where the time goes in v1:
time: 155 us; the launch traced here: 154 us
  blocking collectives  49.8 us (32%)
  starting transfers between devices  32.5 us (21%)
  between operations  26.8 us (17%)
  waiting for transfers between devices  16.9 us (11%)
  other arithmetic  14.6 us (9%)
  local copies, waits for them, and re-layouts  12.3 us (8%)
    all_to_all x1, blocking collectives, exchange_blocks(): received = lax.all_to_all(jnp.stack(cells), axis, 0, 0)  32.9 us
    ppermute x12, starting transfers between devices, from_behind(): return lax.ppermute(x, axis, pairs)  28.9 us
    all_to_all x1, blocking collectives, on_device(): lax.all_to_all(field, 'slab', split_axis=1, concat_axis=2, tiled=True)  16.9 us
    ppermute x12, waiting for transfers between devices, from_behind(): return lax.ppermute(x, axis, pairs)  16.9 us
    unnamed x9, local copies, waits for them, and re-layouts  6.43 us
    all_to_all x1, starting transfers between devices, on_device(): lax.all_to_all(exchange_blocks(volumes, 'slab', 2, 1), 'bin', split_axis=...  3.51 us
  transfers between devices with their start and end apart: 13, of which 6 were waited for; matrix products, arithmetic and copies ran while one was open for 2% of the time, Pallas kernels for 0%

profile of v1, /device:TPU:0, one launch (start us, length us, event | category | flops | bytes accessed | tf_op | source)
XLA Modules:
  0.0 153.8 jit_solution(4720220138608328086)
XLA Ops:
  0.0 0.9 bitcast_dynamic-update-slice_fusion.7
  0.9 0.9 bitcast_dynamic-update-slice_fusion.6
  1.9 0.9 bitcast_dynamic-update-slice_fusion.5
  2.8 0.9 bitcast_dynamic-update-slice_fusion.4
  3.7 0.9 bitcast_dynamic-update-slice_fusion.3
  4.6 0.9 bitcast_dynamic-update-slice_fusion.2
  5.5 0.9 bitcast_dynamic-update-slice_fusion.1
  6.5 0.9 bitcast_dynamic-update-slice_fusion
  7.4 32.9 %all_to_all.35 = f32[8,2,4,8,512]{4,3,2,1,0:T(8,128)S(1)} all-to-all(f32[8,2,4,8,512]{4,3,2,1,0:T(8,128)S(1)} %bitcast_dynamic-update-slice_fusion), channel_id=1, replica_groups=mesh['bin'=4,'slab'=8] {'slab'}, dimensions={0} | all-to-all | bytes 2097152 | tf_op jit(solution)/shard_map/all_to_all | solution.py:11
  40.3 1.1 copy.14
  41.4 3.5 %all-to-all-start.1 = ((f32[2,32,8,512]{3,2,0,1:T(8,128)}), f32[2,32,8,512]{3,2,0,1:T(8,128)S(1)}, u32[]{:S(2)}, u32[]{:S(2)}) async-start(f32[2,32,8,512]{3,2,0,1:T(8,128)} %copy.14), calls=%async_computation.1 | async-start | bytes 2097152 | tf_op jit(solution)/shard_map/all_to_all | solution.py:100
  45.6 0.1 convolution_add_fusion
  45.7 0.7 fusion.20
  72.0 0.8 copy.16
  72.8 0.7 all_to_all.29
  73.5 1.0 convolution_bitcast_fusion
  74.5 0.6 multiply_add_fusion.11
  75.2 0.4 pad_maximum_fusion
  75.5 0.1 slice_subtract_fusion.7
  75.6 0.3 slice_subtract_fusion.2
  76.0 1.3 collective-permute-start.1
  77.4 1.3 collective-permute-start
  78.7 0.4 multiply_reduce_fusion.6
  79.1 3.3 %collective-permute-done.1 = f32[3,8,1,512]{3,0,2,1:T(4,128)S(1)} collective-permute-done((f32[3,8,1,512]{3,0,2,1:T(4,128)S(1)}, f32[3,8,1,512]{3,0,2,1:T(4,128)S(1)}, u32[]{:S(2)}, u32[]{:S(2)}) %collective-permute-start.1) | collective-permute-done | bytes 49184 | tf_op jit(solution)/shard_map/ppermute | solution.py:18
  82.4 0.4 multiply_reduce_fusion.7
  82.8 0.4 multiply_reduce_fusion.8
  83.2 0.5 fusion.12
  83.8 2.6 %collective-permute-start.2 = (f32[3,1,8,512]{3,0,2,1:T(4,128)S(1)}, f32[3,1,8,512]{3,0,2,1:T(4,128)S(1)}, u32[]{:S(2)}, u32[]{:S(2)}) collective-permute-start(f32[3,1,8,512]{3,0,2,1:T(4,128)S(1)} %slice.331), channel_id=1, source_target_pairs={{0,8},{8,16},{16,24},{1,9},{9,17},{17,25},{2,10},{10,18},{18,26},{... | collective-permute-start | bytes 147464 | tf_op jit(solution)/shard_map/ppermute | solution.py:18
  86.4 4.4 %collective-permute-start.3 = (f32[3,8,1,512]{3,0,2,1:T(4,128)S(1)}, f32[3,8,1,512]{3,0,2,1:T(4,128)S(1)}, u32[]{:S(2)}, u32[]{:S(2)}) collective-permute-start(f32[3,8,1,512]{3,0,2,1:T(4,128)S(1)} %slice.333), channel_id=1, source_target_pairs={{0,1},{1,2},{2,3},{3,4},{4,5},{5,6},{6,7},{8,9},{9,10},{10,11},{11... | collective-permute-start | bytes 147464 | tf_op jit(solution)/shard_map/ppermute | solution.py:18
  91.0 2.3 %collective-permute-done.3 = f32[3,8,1,512]{3,0,2,1:T(4,128)S(1)} collective-permute-done((f32[3,8,1,512]{3,0,2,1:T(4,128)S(1)}, f32[3,8,1,512]{3,0,2,1:T(4,128)S(1)}, u32[]{:S(2)}, u32[]{:S(2)}) %collective-permute-start.3) | collective-permute-done | bytes 49184 | tf_op jit(solution)/shard_map/ppermute | solution.py:18
  93.3 0.9 fusion.3
  94.1 0.6 multiply_add_fusion.8
  94.8 0.4 pad_maximum_fusion.3
  95.2 0.1 slice_subtract_fusion.5
  95.3 0.3 slice_subtract_fusion.1
  95.6 1.3 collective-permute-start.5
  96.9 0.1 slice_subtract_fusion.6
  97.0 1.5 collective-permute-start.4
  98.5 3.9 %collective-permute-done.5 = f32[3,8,1,512]{3,0,2,1:T(4,128)S(1)} collective-permute-done((f32[3,8,1,512]{3,0,2,1:T(4,128)S(1)}, f32[3,8,1,512]{3,0,2,1:T(4,128)S(1)}, u32[]{:S(2)}, u32[]{:S(2)}) %collective-permute-start.5) | collective-permute-done | bytes 49184 | tf_op jit(solution)/shard_map/ppermute | solution.py:18
  102.4 1.7 %multiply_reduce_fusion.3 = (f32[8,8,512]{2,1,0:T(8,128)S(1)}, f32[3,8,8,512]{3,0,2,1:T(4,128)S(1)}, f32[8,8,512]{2,1,0:T(8,128)S(1)}, f32[3,8,8,512]{3,0,2,1:T(...) fusion(f32[8,8,512]{2,1,0:T(8,128)S(1)} %maximum_divide_fusion.2, ...), kind=kLoop, calls=%fused_computation.43 | loop fusion | flops 1474560 | bytes 4061696 | tf_op jit(solution)/shard_map/reduce_sum | solution.py:90
  104.2 0.7 multiply_subtract_fusion.3
  105.0 2.3 %collective-permute-start.6 = (f32[3,1,8,512]{3,0,2,1:T(4,128)S(1)}, f32[3,1,8,512]{3,0,2,1:T(4,128)S(1)}, u32[]{:S(2)}, u32[]{:S(2)}) collective-permute-start(f32[3,1,8,512]{3,0,2,1:T(4,128)S(1)} %slice.349), channel_id=1, source_target_pairs={{0,8},{8,16},{16,24},{1,9},{9,17},{17,25},{2,10},{10,18},{18,26},{... | collective-permute-start | bytes 147464 | tf_op jit(solution)/shard_map/ppermute | solution.py:18
  107.3 5.0 %collective-permute-start.7 = (f32[3,8,1,512]{3,0,2,1:T(4,128)S(1)}, f32[3,8,1,512]{3,0,2,1:T(4,128)S(1)}, u32[]{:S(2)}, u32[]{:S(2)}) collective-permute-start(f32[3,8,1,512]{3,0,2,1:T(4,128)S(1)} %slice.351), channel_id=1, source_target_pairs={{0,1},{1,2},{2,3},{3,4},{4,5},{5,6},{6,7},{8,9},{9,10},{10,11},{11... | collective-permute-start | bytes 147464 | tf_op jit(solution)/shard_map/ppermute | solution.py:18
  112.3 0.1 slice.350
  112.4 1.7 %collective-permute-done.7 = f32[3,8,1,512]{3,0,2,1:T(4,128)S(1)} collective-permute-done((f32[3,8,1,512]{3,0,2,1:T(4,128)S(1)}, f32[3,8,1,512]{3,0,2,1:T(4,128)S(1)}, u32[]{:S(2)}, u32[]{:S(2)}) %collective-permute-start.7) | collective-permute-done | bytes 49184 | tf_op jit(solution)/shard_map/ppermute | solution.py:18
  114.1 0.8 fusion.7
  115.0 0.6 multiply_add_fusion.5
  115.6 0.4 pad_maximum_fusion.4
  116.0 0.1 slice_subtract_fusion.3
  116.1 0.3 slice_subtract_fusion
  116.5 1.3 collective-permute-start.9
  117.9 1.3 collective-permute-start.8
  119.2 4.1 %collective-permute-done.9 = f32[3,8,1,512]{3,0,2,1:T(4,128)S(1)} collective-permute-done((f32[3,8,1,512]{3,0,2,1:T(4,128)S(1)}, f32[3,8,1,512]{3,0,2,1:T(4,128)S(1)}, u32[]{:S(2)}, u32[]{:S(2)}) %collective-permute-start.9) | collective-permute-done | bytes 49184 | tf_op jit(solution)/shard_map/ppermute | solution.py:18
  123.3 1.4 multiply_reduce_fusion.1
  124.8 0.7 multiply_subtract_fusion
  125.5 1.5 %collective-permute-start.10 = (f32[3,1,8,512]{3,0,2,1:T(4,128)S(1)}, f32[3,1,8,512]{3,0,2,1:T(4,128)S(1)}, u32[]{:S(2)}, u32[]{:S(2)}) collective-permute-start(f32[3,1,8,512]{3,0,2,1:T(4,128)S(1)} %slice.367), channel_id=1, source_target_pairs={{0,8},{8,16},{16,24},{1,9},{9,17},{17,25},{2,10},{10,18},{18,26},{... | collective-permute-start | bytes 147464 | tf_op jit(solution)/shard_map/ppermute | solution.py:18
  127.1 5.2 %collective-permute-start.11 = (f32[3,8,1,512]{3,0,2,1:T(4,128)S(1)}, f32[3,8,1,512]{3,0,2,1:T(4,128)S(1)}, u32[]{:S(2)}, u32[]{:S(2)}) collective-permute-start(f32[3,8,1,512]{3,0,2,1:T(4,128)S(1)} %slice.369), channel_id=1, source_target_pairs={{0,1},{1,2},{2,3},{3,4},{4,5},{5,6},{6,7},{8,9},{9,10},{10,11},{11... | collective-permute-start | bytes 147464 | tf_op jit(solution)/shard_map/ppermute | solution.py:18
  132.5 1.7 %collective-permute-done.11 = f32[3,8,1,512]{3,0,2,1:T(4,128)S(1)} collective-permute-done((f32[3,8,1,512]{3,0,2,1:T(4,128)S(1)}, f32[3,8,1,512]{3,0,2,1:T(4,128)S(1)}, u32[]{:S(2)}, u32[]{:S(2)}) %collective-permute-start.11) | collective-permute-done | bytes 49184 | tf_op jit(solution)/shard_map/ppermute | solution.py:18
  134.2 0.9 fusion.11
  135.0 0.6 multiply_add_fusion.2
  135.7 0.4 pad_maximum_fusion.5
  136.0 0.1 copy.17
  136.2 16.9 %all_to_all.36 = f32[3,8,8,512]{3,2,0,1:T(8,128)S(1)} all-to-all(f32[3,8,8,512]{3,2,0,1:T(8,128)S(1)} %copy.17), channel_id=1, replica_groups=mesh['bin'=4,'slab'=8] {'slab'}, dimensions={1} | all-to-all | bytes 786432 | tf_op jit(solution)/shard_map/all_to_all | solution.py:116
  153.0 0.8 copy.23
  (38 shorter events, 1.2 us)
Async XLA Ops:
  0.0 45.6 %copy-start = (f32[8,3]{0,1:T(4,128)S(1)}, f32[8,3]{0,1:T(4,128)}, u32[]{:S(2)}) copy-start(f32[8,3]{0,1:T(4,128)} %param.5) | copy-start | bytes 292
  41.4 30.5 %all-to-all-start.1 = ((f32[2,32,8,512]{3,2,0,1:T(8,128)}), f32[2,32,8,512]{3,2,0,1:T(8,128)S(1)}, u32[]{:S(2)}, u32[]{:S(2)}) async-start(f32[2,32,8,512]{3,2,0,1:T(8,128)} %copy.14), calls=%async_computation.1 | async-start | bytes 2097152 | tf_op jit(solution)/shard_map/all_to_all | solution.py:100
  76.0 6.4 %collective-permute-start.1 = (f32[3,8,1,512]{3,0,2,1:T(4,128)S(1)}, f32[3,8,1,512]{3,0,2,1:T(4,128)S(1)}, u32[]{:S(2)}, u32[]{:S(2)}) collective-permute-start(f32[3,8,1,512]{3,0,2,1:T(4,128)S(1)} %slice.327), channel_id=1, source_target_pairs={{1,0},{2,1},{3,2},{4,3},{5,4},{6,5},{7,6},{9,8},{10,9},{11,10},{12... | collective-permute-start | bytes 147464 | tf_op jit(solution)/shard_map/ppermute | solution.py:18
  77.4 5.3 %collective-permute-start = (f32[3,1,8,512]{3,0,2,1:T(4,128)S(1)}, f32[3,1,8,512]{3,0,2,1:T(4,128)S(1)}, u32[]{:S(2)}, u32[]{:S(2)}) collective-permute-start(f32[3,1,8,512]{3,0,2,1:T(4,128)S(1)} %slice.323), channel_id=1, source_target_pairs={{8,0},{16,8},{24,16},{9,1},{17,9},{25,17},{10,2},{18,10},{26,18},{... | collective-permute-start | bytes 147464 | tf_op jit(solution)/shard_map/ppermute | solution.py:18
  83.8 7.2 %collective-permute-start.2 = (f32[3,1,8,512]{3,0,2,1:T(4,128)S(1)}, f32[3,1,8,512]{3,0,2,1:T(4,128)S(1)}, u32[]{:S(2)}, u32[]{:S(2)}) collective-permute-start(f32[3,1,8,512]{3,0,2,1:T(4,128)S(1)} %slice.331), channel_id=1, source_target_pairs={{0,8},{8,16},{16,24},{1,9},{9,17},{17,25},{2,10},{10,18},{18,26},{... | collective-permute-start | bytes 147464 | tf_op jit(solution)/shard_map/ppermute | solution.py:18
  86.4 6.9 %collective-permute-start.3 = (f32[3,8,1,512]{3,0,2,1:T(4,128)S(1)}, f32[3,8,1,512]{3,0,2,1:T(4,128)S(1)}, u32[]{:S(2)}, u32[]{:S(2)}) collective-permute-start(f32[3,8,1,512]{3,0,2,1:T(4,128)S(1)} %slice.333), channel_id=1, source_target_pairs={{0,1},{1,2},{2,3},{3,4},{4,5},{5,6},{6,7},{8,9},{9,10},{10,11},{11... | collective-permute-start | bytes 147464 | tf_op jit(solution)/shard_map/ppermute | solution.py:18
  95.6 6.8 %collective-permute-start.5 = (f32[3,8,1,512]{3,0,2,1:T(4,128)S(1)}, f32[3,8,1,512]{3,0,2,1:T(4,128)S(1)}, u32[]{:S(2)}, u32[]{:S(2)}) collective-permute-start(f32[3,8,1,512]{3,0,2,1:T(4,128)S(1)} %slice.345), channel_id=1, source_target_pairs={{1,0},{2,1},{3,2},{4,3},{5,4},{6,5},{7,6},{9,8},{10,9},{11,10},{12... | collective-permute-start | bytes 147464 | tf_op jit(solution)/shard_map/ppermute | solution.py:18
  97.0 5.4 %collective-permute-start.4 = (f32[3,1,8,512]{3,0,2,1:T(4,128)S(1)}, f32[3,1,8,512]{3,0,2,1:T(4,128)S(1)}, u32[]{:S(2)}, u32[]{:S(2)}) collective-permute-start(f32[3,1,8,512]{3,0,2,1:T(4,128)S(1)} %slice.341), channel_id=1, source_target_pairs={{8,0},{16,8},{24,16},{9,1},{17,9},{25,17},{10,2},{18,10},{26,18},{... | collective-permute-start | bytes 147464 | tf_op jit(solution)/shard_map/ppermute | solution.py:18
  105.0 7.5 %collective-permute-start.6 = (f32[3,1,8,512]{3,0,2,1:T(4,128)S(1)}, f32[3,1,8,512]{3,0,2,1:T(4,128)S(1)}, u32[]{:S(2)}, u32[]{:S(2)}) collective-permute-start(f32[3,1,8,512]{3,0,2,1:T(4,128)S(1)} %slice.349), channel_id=1, source_target_pairs={{0,8},{8,16},{16,24},{1,9},{9,17},{17,25},{2,10},{10,18},{18,26},{... | collective-permute-start | bytes 147464 | tf_op jit(solution)/shard_map/ppermute | solution.py:18
  107.3 6.9 %collective-permute-start.7 = (f32[3,8,1,512]{3,0,2,1:T(4,128)S(1)}, f32[3,8,1,512]{3,0,2,1:T(4,128)S(1)}, u32[]{:S(2)}, u32[]{:S(2)}) collective-permute-start(f32[3,8,1,512]{3,0,2,1:T(4,128)S(1)} %slice.351), channel_id=1, source_target_pairs={{0,1},{1,2},{2,3},{3,4},{4,5},{5,6},{6,7},{8,9},{9,10},{10,11},{11... | collective-permute-start | bytes 147464 | tf_op jit(solution)/shard_map/ppermute | solution.py:18
  116.5 6.8 %collective-permute-start.9 = (f32[3,8,1,512]{3,0,2,1:T(4,128)S(1)}, f32[3,8,1,512]{3,0,2,1:T(4,128)S(1)}, u32[]{:S(2)}, u32[]{:S(2)}) collective-permute-start(f32[3,8,1,512]{3,0,2,1:T(4,128)S(1)} %slice.363), channel_id=1, source_target_pairs={{1,0},{2,1},{3,2},{4,3},{5,4},{6,5},{7,6},{9,8},{10,9},{11,10},{12... | collective-permute-start | bytes 147464 | tf_op jit(solution)/shard_map/ppermute | solution.py:18
  117.9 5.4 %collective-permute-start.8 = (f32[3,1,8,512]{3,0,2,1:T(4,128)S(1)}, f32[3,1,8,512]{3,0,2,1:T(4,128)S(1)}, u32[]{:S(2)}, u32[]{:S(2)}) collective-permute-start(f32[3,1,8,512]{3,0,2,1:T(4,128)S(1)} %slice.359), channel_id=1, source_target_pairs={{8,0},{16,8},{24,16},{9,1},{17,9},{25,17},{10,2},{18,10},{26,18},{... | collective-permute-start | bytes 147464 | tf_op jit(solution)/shard_map/ppermute | solution.py:18
  125.5 6.9 %collective-permute-start.10 = (f32[3,1,8,512]{3,0,2,1:T(4,128)S(1)}, f32[3,1,8,512]{3,0,2,1:T(4,128)S(1)}, u32[]{:S(2)}, u32[]{:S(2)}) collective-permute-start(f32[3,1,8,512]{3,0,2,1:T(4,128)S(1)} %slice.367), channel_id=1, source_target_pairs={{0,8},{8,16},{16,24},{1,9},{9,17},{17,25},{2,10},{10,18},{18,26},{... | collective-permute-start | bytes 147464 | tf_op jit(solution)/shard_map/ppermute | solution.py:18
  127.1 7.1 %collective-permute-start.11 = (f32[3,8,1,512]{3,0,2,1:T(4,128)S(1)}, f32[3,8,1,512]{3,0,2,1:T(4,128)S(1)}, u32[]{:S(2)}, u32[]{:S(2)}) collective-permute-start(f32[3,8,1,512]{3,0,2,1:T(4,128)S(1)} %slice.369), channel_id=1, source_target_pairs={{0,1},{1,2},{2,3},{3,4},{4,5},{5,6},{6,7},{8,9},{9,10},{10,11},{11... | collective-permute-start | bytes 147464 | tf_op jit(solution)/shard_map/ppermute | solution.py:18
